TPU v7x, 256 devices: a whole 4x4x8 slice. The times are simulated.
256 devices in a mesh: shots: 4 (over y), space: 64 (over z, x, core).
Axes of the slice: x: 4, y: 4, z: 8, core: 2. Of those that a mesh axis runs over, the one named last changes fastest.
Arguments:
- probes: bfloat16 [8, 64, 2, 1024, 8, 128], P('shots', None, None, 'space'), may hold values from -6 to 6
- sources: bfloat16 [8, 2, 1024, 8, 128], P('shots', None, 'space'), may hold values from -6 to 6
- sketch: bfloat16 [256, 64, 64], P('space'), may hold values from -6 to 6
- pairing: int32 [8], replicated, may hold values from 0 to 7, each once
Outputs:
- basis: bfloat16 [256, 64, 64], P('space', 'shots')
Inputs may be any that keep to these rules, and one draw needn't show every extreme that they name: `pairing`: a permutation of the 8 shot groups.
All inputs are finite; a program needn't handle non-finite values.
Results may differ from a plain program's by a relative error of at most 0.013.
Values may be sent and summed in bfloat16 or wider, within the bound.
A program may use at most 64 MiB of HBM per device.

v0:
```python
import math

import jax
import jax.numpy as jnp
from jax import lax
from jax.sharding import PartitionSpec as P


def extended(x, sides, width):
    for axis, dim in sides:
        count, length = (lax.axis_size(axis), x.shape[dim])
        up = [(i, (i + 1) % count) for i in range(count - 1)]
        down = [(j, i) for i, j in up]
        last = lax.slice_in_dim(x, length - width, length, axis=dim)
        initial = lax.slice_in_dim(x, 0, width, axis=dim)
        before = lax.ppermute(last, axis, up)
        after = lax.ppermute(initial, axis, down)
        x = jnp.concatenate([before, x, after], axis=dim)
    return x


def from_partner(value, axis, distance):
    mask = 2**distance
    pairs = [(source, source ^ mask) for source in range(lax.axis_size(axis))]
    return lax.ppermute(value, axis, pairs)


def spline_table(fine_count, coarse_count, fine_start, coarse_start):
    fine_pos = jnp.arange(fine_count, dtype=jnp.float32) + fine_start
    coarse_pos = jnp.arange(coarse_count, dtype=jnp.float32) + coarse_start
    distance = jnp.abs((fine_pos[:, None] + 0.5 - 4.0 * coarse_pos[None, :] - 2.0) / 4.0)
    inner_part = 2.0 / 3.0 - distance**2 + 0.5 * distance**3
    outer_part = jnp.maximum(2.0 - distance, 0.0) ** 3 / 6.0
    return jnp.where(distance < 1.0, inner_part, outer_part) / 4.0


def solve_coef(gram_mats, cross_mats):
    rank_size = gram_mats.shape[-1]
    trace_sum = jnp.trace(gram_mats, axis1=1, axis2=2)
    ridge_term = 0.01 * trace_sum / rank_size + 1e-06
    identity = jnp.eye(rank_size, dtype=jnp.float32)
    factor = jnp.linalg.cholesky(gram_mats + ridge_term[:, None, None] * identity)
    halfway = lax.linalg.triangular_solve(factor, cross_mats, left_side=True, lower=True)
    return lax.linalg.triangular_solve(
        factor, halfway, left_side=True, lower=True, transpose_a=True
    )


def merge_level(pieces, sketch, scaling):
    gram_mats = jnp.einsum("pxay,pxby->pab", pieces, pieces, preferred_element_type=jnp.float32)
    cross_mats = jnp.einsum("pxay,xby->pab", pieces, sketch, preferred_element_type=jnp.float32)
    gram_mats, cross_mats = lax.psum((gram_mats, cross_mats), "space")
    coefficients = solve_coef(gram_mats, cross_mats).astype(jnp.bfloat16)
    term_sums = jnp.einsum(
        "pxay,pab->pxby", pieces, coefficients, preferred_element_type=jnp.float32
    )
    pair_count = pieces.shape[0] // 2
    term_sums = term_sums.reshape((pair_count, 2) + term_sums.shape[1:])
    return (scaling * (term_sums[:, 0] + term_sums[:, 1])).astype(jnp.bfloat16)


def body(probes, sources, sketch, pairing):
    hi = lax.Precision.HIGHEST
    groups, rank_size, steps_t, fine_x, fine_y, fine_z = probes.shape
    coarse_x = fine_x // 4
    coarse_y = fine_y // 4
    coarse_z = fine_z // 4
    images = jnp.einsum("gatxyz,gtxyz->gaxyz", probes, sources, preferred_element_type=jnp.float32)
    images = jnp.einsum(
        "gaxyz,zc->gaxyc", images, spline_table(fine_z, coarse_z, 0, 0), precision=hi
    )
    images = jnp.einsum(
        "gaxyc,yd->gaxdc", images, spline_table(fine_y, coarse_y, 0, 0), precision=hi
    )
    images = images.reshape(groups, rank_size, fine_x, coarse_y * coarse_z)
    padded = extended(images, (("space", 2),), 6)
    table_x = spline_table(fine_x + 12, coarse_x, -6, 0)
    coarse = jnp.einsum("gaxc,xe->gaec", padded, table_x, precision=hi)
    leaves = jnp.transpose(coarse, (0, 2, 1, 3)).astype(jnp.bfloat16)
    gathered = lax.all_gather(leaves, "shots", axis=0, tiled=True)
    cell_count = coarse_x * lax.axis_size("space") * coarse_y * coarse_z
    scaling = math.sqrt(cell_count / rank_size)
    shot_index = lax.axis_index("shots")
    first_slot = shot_index * groups
    chosen_ids = lax.dynamic_slice_in_dim(pairing, first_slot, groups)
    chosen = jnp.take(gathered, chosen_ids, axis=0)
    merged = merge_level(chosen, sketch, scaling)[0]
    for bit_number in range(lax.axis_size("shots").bit_length() - 1):
        partner_piece = from_partner(merged, "shots", bit_number)
        upper_bit = shot_index // (1 << bit_number) % 2
        low_piece = jnp.where(upper_bit == 1, partner_piece, merged)
        high_piece = jnp.where(upper_bit == 1, merged, partner_piece)
        merged = merge_level(jnp.stack([low_piece, high_piece]), sketch, scaling)[0]
    column_count = rank_size // lax.axis_size("shots")
    column_start = shot_index * column_count
    return lax.dynamic_slice_in_dim(merged, column_start, column_count, 1)


def solution(mesh):
    in_specs = (
        P("shots", None, None, "space", None, None),
        P("shots", None, "space", None, None),
        P("space", None, None),
        P(),
    )
    out_specs = P("space", "shots", None)
    return jax.shard_map(body, mesh=mesh, in_specs=in_specs, out_specs=out_specs, check_vma=False)
```

profile of v0, /device:TPU:1, one launch (start us, length us, event | category | flops | bytes accessed | tf_op | source)
XLA Modules:
  0.0 711.2 jit_solution(15676026081524795223)
XLA Ops:
  7.5 10.0 %multiply_reduce_fusion = f32[2,16,8,128,64]{3,2,1,4,0:T(8,128)} fusion(f32[2,16,8,128,2]{3,2,1,4,0:T(8,128)S(1)} %bitcast_convert_fusion, bf16[2,64,2,16,8,128]{5,4,3,2,1,0:T(8,128)(2,1)} %param.9), kind=kLoop, calls=%fused_computation.1 | loop fusion | flops 10485760 | bytes 17039360
  17.5 28.1 %fusion = f32[2,64,16,8,32]{1,4,3,2,0:T(8,128)S(1)} fusion(f32[2,16,8,128,64]{3,2,1,4,0:T(8,128)} %multiply_reduce_fusion, f32[32]{0:T(128)S(1)} %iota_multiply_fusion, f32[128]{0:T(128)S(1)} %iota_add_fusion), kind=kOutput, calls=%fused_computation.2 | convolution fusion | flops 805376000 | bytes 10486400 | tf_op jit(solution)/shard_map/gaxyz,zc->gaxyc/dot_general | solution.py:69
  45.6 5.5 fusion.11
  51.8 5.1 collective-permute-start.1
  56.9 1.9 collective-permute-start
  59.1 4.1 collective-permute-done.1
  63.2 1.8 collective-permute-done
  65.0 1.4 fusion.17
  66.4 11.1 %all_gather.3 = bf16[8,4,64,64]{3,2,1,0:T(8,128)(2,1)S(1)} all-gather(bf16[2,4,64,64]{3,2,1,0:T(8,128)(2,1)S(1)} %copy.59), channel_id=1, replica_groups=mesh['shots'=4,'space'=64] {'shots'}, dimensions={0}, use_global_device_ids=true | all-gather | bytes 327680 | tf_op jit(solution)/shard_map/all_gather | solution.py:80
  79.9 183.8 %all-reduce.11.cloned.1.call-done = (f32[2,64,64]{2,1,0:T(8,128)}, f32[2,64,64]{1,2,0:T(8,128)}) async-done(((f32[2,64,64]{2,1,0:T(8,128)}, f32[2,64,64]{1,2,0:T(8,128)}), (f32[2,64,64]{2,1,0:T(8,128)}, f32[2,64,64]{1,2,0:T(8,128)})) %all-reduce.11.cloned.1.call-update) | async-done | bytes 65552 | tf_op jit(solution)/shard_map/psum | solution.py:52
  266.6 11.7 %custom-call.15 = f32[2,64,64]{2,1,0:T(8,128)S(1)} custom-call(f32[2,64,64]{2,1,0:T(8,128)S(1)} %fusion.43), custom_call_target="Cholesky" | custom-call | tf_op jit(solution)/shard_map/jit(cholesky)/cholesky | solution.py:42
  278.6 9.8 %custom-call.17 = f32[2,1,64,64]{2,3,1,0:T(8,128)S(1)} custom-call(f32[2,1,64,64]{3,2,1,0:T(8,128)S(1)} %select_bitcast_fusion.2), custom_call_target="InvertDiagBlocksLowerTriangular" | custom-call | tf_op jit(solution)/shard_map/triangular_solve/custom-call.2 | solution.py:44
  288.4 1.1 fusion.40
  290.0 1.3 collective-permute-start.2
  291.3 2.2 collective-permute-done.2
  295.2 174.8 %all-reduce.9.cloned.1.call-done = (f32[2,64,64]{2,1,0:T(8,128)}, f32[2,64,64]{1,2,0:T(8,128)}) async-done(((f32[2,64,64]{2,1,0:T(8,128)}, f32[2,64,64]{1,2,0:T(8,128)}), (f32[2,64,64]{2,1,0:T(8,128)}, f32[2,64,64]{1,2,0:T(8,128)})) %all-reduce.9.cloned.1.call-update) | async-done | bytes 65552 | tf_op jit(solution)/shard_map/psum | solution.py:52
  472.9 11.7 %custom-call.18 = f32[2,64,64]{2,1,0:T(8,128)S(1)} custom-call(f32[2,64,64]{2,1,0:T(8,128)S(1)} %fusion.36), custom_call_target="Cholesky" | custom-call | tf_op jit(solution)/shard_map/jit(cholesky)/cholesky | solution.py:42
  484.9 9.8 %custom-call.20 = f32[2,1,64,64]{2,3,1,0:T(8,128)S(1)} custom-call(f32[2,1,64,64]{3,2,1,0:T(8,128)S(1)} %select_bitcast_fusion.1), custom_call_target="InvertDiagBlocksLowerTriangular" | custom-call | tf_op jit(solution)/shard_map/triangular_solve/custom-call.2 | solution.py:44
  494.7 1.1 fusion.33
  496.3 2.8 collective-permute-start.3
  499.1 2.2 collective-permute-done.3
  502.9 174.9 %all-reduce.7.cloned.1.call-done = (f32[2,64,64]{2,1,0:T(8,128)}, f32[2,64,64]{1,2,0:T(8,128)}) async-done(((f32[2,64,64]{2,1,0:T(8,128)}, f32[2,64,64]{1,2,0:T(8,128)}), (f32[2,64,64]{2,1,0:T(8,128)}, f32[2,64,64]{1,2,0:T(8,128)})) %all-reduce.7.cloned.1.call-update) | async-done | bytes 65552 | tf_op jit(solution)/shard_map/psum | solution.py:52
  680.7 11.7 %custom-call.21 = f32[2,64,64]{2,1,0:T(8,128)S(1)} custom-call(f32[2,64,64]{2,1,0:T(8,128)S(1)} %fusion.32), custom_call_target="Cholesky" | custom-call | tf_op jit(solution)/shard_map/jit(cholesky)/cholesky | solution.py:42
  692.6 9.8 %custom-call.23 = f32[2,1,64,64]{2,3,1,0:T(8,128)S(1)} custom-call(f32[2,1,64,64]{3,2,1,0:T(8,128)S(1)} %select_bitcast_fusion), custom_call_target="InvertDiagBlocksLowerTriangular" | custom-call | tf_op jit(solution)/shard_map/triangular_solve/custom-call.2 | solution.py:44
  (71 shorter events, 19.9 us)
Async XLA Ops:
  6.5 72.4 %copy-start = (bf16[4,64,64]{2,1,0:T(8,128)(2,1)S(1)}, bf16[4,64,64]{2,1,0:T(8,128)(2,1)}, u32[]{:S(2)}) copy-start(bf16[4,64,64]{2,1,0:T(8,128)(2,1)} %param.11) | copy-start | bytes 98308
  6.5 257.2 %all-reduce.11.cloned.1.call-start = ((), (), s32[]{:S(2)}) async-start(), calls=%async_computation.2 | async-start | bytes 262144 | tf_op jit(solution)/shard_map/psum | solution.py:52
  51.1 7.8 %copy-start.1 = (s32[8]{0:T(128)S(1)}, s32[8]{0:T(128)}, u32[]{:S(2)}) copy-start(s32[8]{0:T(128)} %param.12) | copy-start | bytes 100
  51.8 11.4 %collective-permute-start.1 = (f32[2,64,6,64]{3,2,1,0:T(8,128)S(1)}, f32[2,64,6,64]{3,2,1,0:T(8,128)S(1)}, u32[]{:S(2)}, u32[]{:S(2)}) collective-permute-start(f32[2,64,6,64]{3,2,1,0:T(8,128)S(1)} %get-tuple-element.17), channel_id=1, source_target_pairs={{1,0},{2,1},{3,2},{4,3},{5,4},{6,5},{7,6},{8,7},{9,8},{10,9},{11,1... | collective-permute-start | bytes 589832 | tf_op jit(solution)/shard_map/ppermute | solution.py:17
  56.9 8.0 %collective-permute-start = (f32[2,64,6,64]{3,2,1,0:T(8,128)S(1)}, f32[2,64,6,64]{3,2,1,0:T(8,128)S(1)}, u32[]{:S(2)}, u32[]{:S(2)}) collective-permute-start(f32[2,64,6,64]{3,2,1,0:T(8,128)S(1)} %get-tuple-element.16), channel_id=1, source_target_pairs={{0,1},{1,2},{2,3},{3,4},{4,5},{5,6},{6,7},{7,8},{8,9},{9,10},{10,1... | collective-permute-start | bytes 589832 | tf_op jit(solution)/shard_map/ppermute | solution.py:16
  79.8 390.2 %all-reduce.9.cloned.1.call-start = ((), (), s32[]{:S(2)}) async-start(), calls=%async_computation.1 | async-start | bytes 262144 | tf_op jit(solution)/shard_map/psum | solution.py:52
  290.0 3.5 collective-permute-start.2
  295.1 382.6 %all-reduce.7.cloned.1.call-start = ((), (), s32[]{:S(2)}) async-start(), calls=%async_computation | async-start | bytes 262144 | tf_op jit(solution)/shard_map/psum | solution.py:52
  496.3 5.0 collective-permute-start.3
Sparse Core Ops, SparseCore 0:
  80.0 183.7 all-reduce.10
  295.3 174.6 all-reduce.8
  503.0 174.6 all-reduce.6
where the time goes:
time: 712 us; the launch traced here: 711 us
  waiting for transfers between devices  544 us (76%)
  other arithmetic  85.6 us (12%)
  matrix products  44.5 us (6%)
  between operations  13.4 us (2%)
  starting transfers between devices  11.2 us (2%)
  blocking collectives  11.1 us (2%)
    psum x3, waiting for transfers between devices, merge_level(): gram_mats, cross_mats = lax.psum((gram_mats, cross_mats), 'space')  533 us
    another operation x10, other arithmetic, solve_coef(): jnp.linalg.cholesky(gram_mats + ridge_term[:, None, None] * identity)  35.6 us
    another operation x7, other arithmetic, solve_coef(): lax.linalg.triangular_solve(factor, halfway, left_side=True, lower=True,...  29.8 us
    dot_general x1, matrix products, body(): jnp.einsum('gaxyz,zc->gaxyc', images, spline_table(fine_z, coarse_z, 0, 0...  28.1 us
  transfers between devices with their start and end apart: 7, of which 7 were waited for; matrix products, arithmetic and copies ran while one was open for 0% of the time, Pallas kernels for 0%

commit v1 on v0

v1 whole, which is shorter than its diff:
```python
import functools
import math

import jax
import jax.numpy as jnp
import numpy as np
from jax import lax
from jax.experimental import pallas as pl
from jax.experimental.pallas import tpu as pltpu
from jax.sharding import PartitionSpec as P

MESH = pl.DeviceIdType.MESH
F32 = jnp.float32
BF16 = jnp.bfloat16
HI = lax.Precision.HIGHEST
RANK = 64
LANES = 128


def spline_weight(distance):
    s = np.abs(distance / 4.0)
    inner = 2.0 / 3.0 - s**2 + 0.5 * s**3
    outer = np.maximum(2.0 - s, 0.0) ** 3 / 6.0
    return np.where(s < 1.0, inner, outer) / 4.0


def weight_tables(fine_x, fine_y, fine_z):
    coarse_x, coarse_y, coarse_z = fine_x // 4 + 4, fine_y // 4, fine_z // 4
    jx, jy, jz = np.arange(fine_x), np.arange(fine_y), np.arange(fine_z)
    ix, iy, iz = np.arange(coarse_x) - 2, np.arange(coarse_y), np.arange(coarse_z)
    wx = spline_weight(jx[None, :] + 0.5 - 4 * ix[:, None] - 2)
    wy = spline_weight(jy[None, :] + 0.5 - 4 * iy[:, None] - 2)
    wz = spline_weight(jz[:, None] + 0.5 - 4 * iz[None, :] - 2)
    wxy = np.einsum("ij,de->idje", wx, wy).reshape(coarse_x * coarse_y, fine_x * fine_y)
    wxy = np.concatenate([wxy, wxy], axis=1).astype(np.float32)
    high = wxy.astype(BF16)
    low = (wxy - high.astype(np.float32)).astype(BF16)
    side = 8
    block = np.zeros((side, fine_z, side, coarse_z), np.float32)
    for i in range(side):
        block[i, :, i, :] = wz
    block = block.reshape(side * fine_z, side * coarse_z).astype(BF16)
    return np.concatenate([high, low], axis=0), block


def restrict_kernel(p_ref, s_ref, wxy_ref, wz_ref, own_ref, up_ref, down_ref, t_ref):
    step = pl.program_id(1)
    chunk = p_ref.shape[1]
    src = s_ref[0].reshape(256, LANES)
    wxy = wxy_ref[...]
    for a in range(0, chunk, 2):
        left = p_ref[0, a].reshape(256, LANES) * src
        right = p_ref[0, a + 1].reshape(256, LANES) * src
        both = jnp.dot(wxy, jnp.concatenate([left, right], axis=1), preferred_element_type=F32)
        both = both[:16] + both[16:]
        row = pl.multiple_of((step * chunk + a) * 16, 32)
        t_ref[pl.ds(row, 16), :] = both[:, :LANES]
        t_ref[pl.ds(row + 16, 16), :] = both[:, LANES:]

    @pl.when(step == pl.num_programs(1) - 1)
    def _():
        wz = wz_ref[...]
        for half in range(2):
            parts = [t_ref[pl.ds(half * 8 + k, RANK, stride=16), :] for k in range(8)]
            x = jnp.concatenate([q.astype(BF16) for q in parts], axis=1)
            y = jnp.dot(x, wz, preferred_element_type=F32)
            if half == 0:
                down_ref[0] = y[:, :LANES].astype(BF16)
                own_ref[0, :, :LANES] = y[:, LANES:]
            else:
                own_ref[0, :, LANES:] = y[:, :LANES]
                up_ref[0] = y[:, LANES:].astype(BF16)


def nt(a, b, precision=None):
    return lax.dot_general(
        a, b, (((1,), (1,)), ((), ())), precision=precision, preferred_element_type=F32
    )


def exchange_kernel(
    shots, depth, owners,
    own_ref, up_ref, down_ref, sk_ref, pair_ref,
    all_ref, g_ref,
    halo, m_ref, rs, red, zb, fin,
    hs, hr, ys, yr, rss, rsr, zs, zr, gs, gr,
):
    me = lax.axis_index("shots")
    sp = lax.axis_index("space")
    count = depth * owners
    z = sp // owners
    o = lax.rem(sp, owners)
    right = lax.rem(sp + 1, count)
    left = lax.rem(sp + count - 1, count)
    group = shots * owners
    line = me * owners + o
    rows = 256 // owners

    barrier = pltpu.get_barrier_semaphore()
    for peer in (left, right):
        pl.semaphore_signal(barrier, inc=1, device_id=(me, peer), device_id_type=MESH)
    for d in range(1, depth):
        peer = lax.rem(z + d, depth) * owners + o
        pl.semaphore_signal(barrier, inc=1, device_id=(me, peer), device_id_type=MESH)
    for d in range(1, group):
        peer = lax.rem(line + d, group)
        pl.semaphore_signal(
            barrier,
            inc=1,
            device_id=(peer // owners, z * owners + lax.rem(peer, owners)),
            device_id_type=MESH,
        )
    pl.semaphore_wait(barrier, 2 + depth - 1 + group - 1)

    def send(src, dst, ssem, rsem, target):
        copy = pltpu.make_async_remote_copy(
            src_ref=src, dst_ref=dst, send_sem=ssem, recv_sem=rsem,
            device_id=target, device_id_type=MESH,
        )
        copy.start()
        return copy

    copies = [
        send(up_ref, halo.at[0], hs.at[0], hr.at[0], (me, right)),
        send(down_ref, halo.at[1], hs.at[1], hr.at[1], (me, left)),
    ]
    for c in copies:
        c.wait()
    below = jnp.where(sp > 0, halo[0].astype(F32), 0.0)
    above = jnp.where(sp < count - 1, halo[1].astype(F32), 0.0)
    lead = (own_ref[:, :, :LANES] + below).astype(BF16)
    tail = (own_ref[:, :, LANES:] + above).astype(BF16)
    all_ref[pl.ds(2 * me, 2), :, :LANES] = lead
    all_ref[pl.ds(2 * me, 2), :, LANES:] = tail

    copies = []
    for d in range(1, shots):
        peer = lax.rem(me + d, shots)
        mine = all_ref.at[pl.ds(2 * me, 2)]
        copies.append(send(mine, mine, ys.at[d - 1], yr.at[d - 1], (peer, sp)))
    for c in copies:
        c.wait()

    half = me // 2
    odd = lax.rem(me, 2)
    base = 4 * half
    p0 = all_ref[pair_ref[base + 2 * odd]]
    p1 = all_ref[pair_ref[base + 2 * odd + 1]]
    xx = all_ref[pair_ref[base + 2 + odd]]
    q0 = all_ref[pair_ref[base]]
    q1 = all_ref[pair_ref[base + 1]]
    sk = sk_ref[...]
    m_ref[0:64, :] = nt(p0, jnp.concatenate([p0, sk], axis=0))
    m_ref[64:128, :] = nt(p1, jnp.concatenate([p1, sk], axis=0))
    m_ref[128:192, :] = nt(xx, jnp.concatenate([q0, q1], axis=0))
    m_ref[192:256, :] = jnp.concatenate([nt(p0, p1), nt(p1, p0)], axis=1)

    copies = []
    for d in range(1, owners):
        peer = lax.rem(o + d, owners)
        copies.append(
            send(
                m_ref.at[pl.ds(pl.multiple_of(peer * rows, rows), rows)],
                rs.at[o], rss.at[d - 1], rsr.at[d - 1], (me, z * owners + peer),
            )
        )
    rs[o] = m_ref[pl.ds(pl.multiple_of(o * rows, rows), rows), :]
    for c in copies:
        c.wait()
    total = rs[0]
    for k in range(1, owners):
        total = total + rs[k]
    red[...] = total
    copies = []
    for d in range(1, depth):
        peer = lax.rem(z + d, depth) * owners + o
        copies.append(send(red, zb.at[z], zs.at[d - 1], zr.at[d - 1], (me, peer)))
    zb[z] = total
    for c in copies:
        c.wait()
    total = zb[0]
    for k in range(1, depth):
        total = total + zb[k]
    fin[...] = total
    copies = []
    for d in range(1, group):
        peer = lax.rem(line + d, group)
        target = (peer // owners, z * owners + lax.rem(peer, owners))
        copies.append(send(fin, g_ref.at[line], gs.at[d - 1], gr.at[d - 1], target))
    g_ref[line] = total
    for c in copies:
        c.wait()


def eliminate(mats):
    sub = lax.broadcasted_iota(jnp.int32, (8, LANES), 0)
    width = 4
    for kb in range(0, RANK, width):
        v0, off = kb // 8, kb % 8
        for w in mats:
            cols = [
                [jnp.broadcast_to(w[v][:, kb + j : kb + j + 1], (8, LANES)) for v in range(8)]
                for j in range(width)
            ]
            r = [jnp.broadcast_to(w[v0][off + i : off + i + 1, :], (8, LANES)) for i in range(width)]
            e = [
                [jnp.broadcast_to(cols[j][v0][off + i : off + i + 1, :], (8, LANES)) for j in range(width)]
                for i in range(width)
            ]
            for i in range(width):
                inv = 1.0 / e[i][i]
                r[i] = r[i] * inv
                for j in range(i + 1, width):
                    e[i][j] = e[i][j] * inv
                for k in range(width):
                    if k != i:
                        f = e[k][i]
                        r[k] = r[k] - f * r[i]
                        for j in range(i + 1, width):
                            e[k][j] = e[k][j] - f * e[i][j]
            for v in range(8):
                new = w[v]
                for j in range(width):
                    new = new - cols[j][v] * r[j]
                if v == v0:
                    for i in range(width):
                        new = jnp.where(sub == off + i, r[i], new)
                w[v] = new


def solve_all(mats):
    row = lax.broadcasted_iota(jnp.int32, (RANK, LANES), 0)
    lane = lax.broadcasted_iota(jnp.int32, (RANK, LANES), 1)
    diagonal = row == lane
    work = []
    for w in mats:
        trace = jnp.sum(jnp.where(diagonal, w, 0.0))
        ridge = 0.01 * trace / RANK + 1e-06
        w = jnp.where(diagonal, w + ridge, w)
        work.append([w[8 * v : 8 * v + 8] for v in range(8)])
    eliminate(work)
    out = []
    for w in work:
        full = jnp.concatenate(w, axis=0)
        full = full.astype(BF16).astype(F32)
        out.append(jnp.transpose(full)[RANK:])
    return out


def tree_kernel(scaling, all_ref, g_ref, pair_ref, out_ref, u_ref):
    me = lax.axis_index("shots")
    twice = scaling * scaling
    eights = [g_ref[p // 2, 64 * (p % 2) : 64 * (p % 2) + 64, :] for p in range(8)]
    first = solve_all(eights)
    second_in, pair_cols, crosses = [], [], []
    for m in range(4):
        c = jnp.concatenate([first[2 * m], first[2 * m + 1]], axis=1)
        a0, a1 = eights[2 * m], eights[2 * m + 1]
        mix = g_ref[m, 192:256, :]
        h = jnp.concatenate(
            [
                jnp.concatenate([a0[:, :RANK], mix[:, :RANK]], axis=1),
                jnp.concatenate([mix[:, RANK:], a1[:, :RANK]], axis=1),
            ],
            axis=0,
        )
        x = jnp.concatenate([a0[:, RANK:], a1[:, RANK:]], axis=0)
        gm = nt(nt(c, h, HI), c, HI)
        xm = jnp.dot(c, x, precision=HI, preferred_element_type=F32)
        second_in.append(jnp.concatenate([twice * gm, scaling * xm], axis=1))
        pair_cols.append(c)
    second = solve_all(second_in)
    third_in, quad_cols = [], []
    for h in range(2):
        d = jnp.concatenate([second[2 * h], second[2 * h + 1]], axis=1)
        c0, c1 = pair_cols[2 * h], pair_cols[2 * h + 1]
        k = jnp.concatenate([g_ref[2 * h, 128:192, :], g_ref[2 * h + 1, 128:192, :]], axis=0)
        g01 = twice * nt(nt(c0, k, HI), c1, HI)
        g10 = twice * nt(jnp.dot(c1, k, precision=HI, preferred_element_type=F32), c0, HI)
        b0, b1 = second_in[2 * h], second_in[2 * h + 1]
        hm = jnp.concatenate(
            [
                jnp.concatenate([b0[:, :RANK], g01], axis=1),
                jnp.concatenate([g10, b1[:, :RANK]], axis=1),
            ],
            axis=0,
        )
        x = jnp.concatenate([b0[:, RANK:], b1[:, RANK:]], axis=0)
        gm = nt(nt(d, hm, HI), d, HI)
        xm = jnp.dot(d, x, precision=HI, preferred_element_type=F32)
        third_in.append(jnp.concatenate([twice * gm, scaling * xm], axis=1))
        e0 = jnp.dot(second[2 * h], c0, precision=HI, preferred_element_type=F32)
        e1 = jnp.dot(second[2 * h + 1], c1, precision=HI, preferred_element_type=F32)
        quad_cols.append(jnp.concatenate([e0, e1], axis=1) * twice)
    third = solve_all(third_in)
    parts = [
        jnp.dot(third[h], quad_cols[h], precision=HI, preferred_element_type=F32) * scaling
        for h in range(2)
    ]
    u_ref[...] = jnp.concatenate(parts, axis=1)
    count = out_ref.shape[1]
    u = u_ref[pl.ds(pl.multiple_of(me * count, count), count), :].astype(BF16)
    total = None
    for p in range(8):
        term = jnp.dot(
            u[:, RANK * p : RANK * p + RANK], all_ref[pair_ref[p]], preferred_element_type=F32
        )
        total = term if total is None else total + term
    for x in range(out_ref.shape[0]):
        out_ref[x] = total[:, RANK * x : RANK * x + RANK].astype(BF16)


def body(depth, probes, sources, sketch, pairing):
    groups, rank, steps, fine_x, fine_y, fine_z = probes.shape
    shots = lax.axis_size("shots")
    space = lax.axis_size("space")
    owners = space // depth
    wxy, wz = weight_tables(fine_x, fine_y, fine_z)
    fine_xy = fine_x * fine_y
    chunk = 16
    vmem = pl.BlockSpec(memory_space=pltpu.VMEM)
    smem = pl.BlockSpec(memory_space=pltpu.SMEM)
    own, up, down = pl.pallas_call(
        restrict_kernel,
        grid=(groups, rank // chunk),
        in_specs=[
            pl.BlockSpec((1, chunk, steps, fine_xy, fine_z), lambda g, a: (g, a, 0, 0, 0)),
            pl.BlockSpec((1, steps, fine_xy, fine_z), lambda g, a: (g, 0, 0, 0)),
            pl.BlockSpec(wxy.shape, lambda g, a: (0, 0)),
            pl.BlockSpec(wz.shape, lambda g, a: (0, 0)),
        ],
        out_specs=[
            pl.BlockSpec((1, rank, 256), lambda g, a: (g, 0, 0)),
            pl.BlockSpec((1, rank, LANES), lambda g, a: (g, 0, 0)),
            pl.BlockSpec((1, rank, LANES), lambda g, a: (g, 0, 0)),
        ],
        out_shape=[
            jax.ShapeDtypeStruct((groups, rank, 256), F32),
            jax.ShapeDtypeStruct((groups, rank, LANES), BF16),
            jax.ShapeDtypeStruct((groups, rank, LANES), BF16),
        ],
        scratch_shapes=[pltpu.VMEM((rank * 16, LANES), F32)],
        name="restrict",
    )(
        probes.reshape(groups, rank, steps, fine_xy, fine_z),
        sources.reshape(groups, steps, fine_xy, fine_z),
        jnp.asarray(wxy),
        jnp.asarray(wz),
    )
    sk = jnp.transpose(sketch, (1, 0, 2)).reshape(rank, 256)
    rows = 256 // owners
    group = shots * owners
    dma = pltpu.SemaphoreType.DMA
    leaves, grams = pl.pallas_call(
        functools.partial(exchange_kernel, shots, depth, owners),
        in_specs=[vmem, vmem, vmem, vmem, smem],
        out_specs=[vmem, vmem],
        out_shape=[
            jax.ShapeDtypeStruct((groups * shots, rank, 256), BF16),
            jax.ShapeDtypeStruct((group, rows, LANES), F32),
        ],
        scratch_shapes=[
            pltpu.VMEM((2, groups, rank, LANES), BF16),
            pltpu.VMEM((256, LANES), F32),
            pltpu.VMEM((owners, rows, LANES), F32),
            pltpu.VMEM((rows, LANES), F32),
            pltpu.VMEM((depth, rows, LANES), F32),
            pltpu.VMEM((rows, LANES), F32),
            dma((2,)), dma((2,)),
            dma((shots - 1,)), dma((shots - 1,)),
            dma((owners - 1,)), dma((owners - 1,)),
            dma((depth - 1,)), dma((depth - 1,)),
            dma((group - 1,)), dma((group - 1,)),
        ],
        compiler_params=pltpu.CompilerParams(collective_id=0, has_side_effects=True),
        name="exchange",
    )(own, up, down, sk, pairing)
    scaling = math.sqrt(fine_x // 4 * space * 64 / rank)
    return pl.pallas_call(
        functools.partial(tree_kernel, scaling),
        in_specs=[vmem, vmem, smem],
        out_specs=vmem,
        out_shape=jax.ShapeDtypeStruct((fine_x // 4, rank // shots, 64), BF16),
        scratch_shapes=[pltpu.VMEM((rank, groups * shots * rank), F32)],
        name="tree",
    )(leaves, grams.reshape(shots, 256, LANES), pairing)


def solution(mesh):
    in_specs = (
        P("shots", None, None, "space", None, None),
        P("shots", None, "space", None, None),
        P("space", None, None),
        P(),
    )
    out_specs = P("space", "shots", None)
    depth = 8 if mesh.shape["space"] == 64 else 2
    return jax.shard_map(
        functools.partial(body, depth),
        mesh=mesh, in_specs=in_specs, out_specs=out_specs, check_vma=False,
    )
```

time: 712 us -> 73.6 us (0.10)
  waiting for transfers between devices: 544 us -> 0 us
  other arithmetic: 85.6 us -> 0 us
  Pallas kernels: 0 us -> 71.6 us
  matrix products: 44.5 us -> 0 us
  between operations: 13.4 us -> 0.01 us
  starting transfers between devices: 11.2 us -> 0 us
  blocking collectives: 11.1 us -> 0 us
    psum x3 -> x0, waiting for transfers between devices: 533 us -> none  [merge_level(): gram_mats, cross_mats = lax.psum((gram_mats, cross_mats), 'space')]
    pallas_call x0 -> x3, Pallas kernels: none -> 71.6 us  [the longest x1 39.1 us: body(): pl.pallas_call(functools.partial(exchange_kernel, shots, depth, owners),...]
    another operation x19 -> x0, other arithmetic: 65.5 us -> none  [the longest x10 35.6 us: solve_coef(): jnp.linalg.cholesky(gram_mats + ridge_term[:, None, None] * identity)]
    dot_general x12 -> x0, matrix products: 40.5 us -> none  [the longest x1 28.1 us: body(): jnp.einsum('gaxyz,zc->gaxyc', images, spline_table(fine_z, coarse_z, 0, 0...]
    ppermute x4 -> x0, starting transfers between devices: 11.1 us -> none  [the longest x1 5.11 us: extended(): after = lax.ppermute(initial, axis, down)]
    all_gather x1 -> x0, blocking collectives: 11.1 us -> none  [body(): gathered = lax.all_gather(leaves, 'shots', axis=0, tiled=True)]
    unnamed x2 -> x0, other arithmetic: 10.9 us -> none
    ppermute x4 -> x0, waiting for transfers between devices: 10.2 us -> none  [the longest x2 4.33 us: from_partner(): return lax.ppermute(value, axis, pairs)]
  transfers between devices with their start and end apart: 7 -> 0, of which waited for: 7 -> 0; matrix products, arithmetic and copies ran while one was open for 0% -> 0% of each run, Pallas kernels for 0% -> 0%
where the time goes in v1:
time: 73.6 us; the launch traced here: 73.2 us
  Pallas kernels  71.6 us (97%)
  local copies, waits for them, and re-layouts  1.61 us (2%)
    pallas_call x1, Pallas kernels, body(): pl.pallas_call(functools.partial(exchange_kernel, shots, depth, owners),...  39.1 us
    pallas_call x1, Pallas kernels, body(): pl.pallas_call(functools.partial(tree_kernel, scaling), in_specs=[vmem, v...  24.5 us
    pallas_call x1, Pallas kernels, body(): pl.pallas_call(restrict_kernel, grid=(groups, rank // chunk), in_specs=[p...  8.08 us

profile of v1, /device:TPU:1, one launch (start us, length us, event | category | flops | bytes accessed | tf_op | source)
XLA Modules:
  0.0 73.2 jit_solution(15987480176547346599)
XLA Ops:
  0.0 0.9 %copy.7 = bf16[64,4,64]{2,1,0:T(4,128)(2,1)S(1)} copy(bf16[64,4,64]{2,0,1:T(8,128)(2,1)} %bitcast.7) | data formatting | bytes 65536 | tf_op jit(solution)/shard_map/transpose | solution.py:350
  0.9 0.7 reshape.14.sk_ref
  1.6 8.1 %restrict.1 = (f32[2,64,256]{2,1,0:T(8,128)}, bf16[2,64,128]{2,1,0:T(8,128)(2,1)}, bf16[2,64,128]{2,1,0:T(8,128)(2,1)}) custom-call(bf16[2,64,2,128,128]{4,3,2,1,0:T(8,128)(2,1)} %bitcast.4, bf16[2,2,128,128]{3,2,1,0:T(8,128)(2,1)} %bitcast.6, bf16[32,256]{1,0:T(8,128)(2,1)} %constant.4.clone.wxy_ref, bf16[1024,256]{1,0:T(8,128)(2,1)} %constant.5.clone.wz_ref), custom_call_target="tpu_custom_call" | custom-call | tf_op jit(solution)/shard_map/restrict/pallas_call | solution.py:323
  9.7 39.1 %exchange.1 = (bf16[8,64,256]{2,1,0:T(8,128)(2,1)}, f32[32,32,128]{2,1,0:T(8,128)}) custom-call(f32[2,64,256]{2,1,0:T(8,128)} %get-tuple-element.10.own_ref, bf16[2,64,128]{2,1,0:T(8,128)(2,1)} %get-tuple-element.11.up_ref, bf16[2,64,128]{2,1,0:T(8,128)(2,1)} %get-tuple-element.12.down_ref, bf16[64,256]{1,0:T(8,128)(2,1)} %reshape.14.sk_ref, s32[8]{0:T(128)} %pair_ref.3), custom_call_target="tpu_custom_call" | custom-call | tf_op jit(solution)/shard_map/exchange/pallas_call | solution.py:354
  48.8 24.5 %tree.1 = bf16[4,16,64]{2,1,0:T(8,128)(2,1)} custom-call(bf16[8,64,256]{2,1,0:T(8,128)(2,1)} %get-tuple-element.13.all_ref, f32[4,256,128]{2,1,0:T(8,128)} %bitcast.5, s32[8]{0:T(128)} %pair_ref.3), custom_call_target="tpu_custom_call" | custom-call | tf_op jit(solution)/shard_map/tree/pallas_call | solution.py:379

commit v2 on v0

v2 whole, which is shorter than its diff:
```python
import functools
import math

import jax
import jax.numpy as jnp
import numpy as np
from jax import lax
from jax.experimental import pallas as pl
from jax.experimental.pallas import tpu as pltpu
from jax.sharding import PartitionSpec as P

MESH = pl.DeviceIdType.MESH
F32 = jnp.float32
BF16 = jnp.bfloat16
HI = lax.Precision.HIGHEST
RANK = 64
LANES = 128


def spline_weight(distance):
    s = np.abs(distance / 4.0)
    inner = 2.0 / 3.0 - s**2 + 0.5 * s**3
    outer = np.maximum(2.0 - s, 0.0) ** 3 / 6.0
    return np.where(s < 1.0, inner, outer) / 4.0


def weight_tables(fine_x, fine_y, fine_z):
    coarse_x, coarse_y, coarse_z = fine_x // 4 + 4, fine_y // 4, fine_z // 4
    jx, jy, jz = np.arange(fine_x), np.arange(fine_y), np.arange(fine_z)
    ix, iy, iz = np.arange(coarse_x) - 2, np.arange(coarse_y), np.arange(coarse_z)
    wx = spline_weight(jx[None, :] + 0.5 - 4 * ix[:, None] - 2)
    wy = spline_weight(jy[None, :] + 0.5 - 4 * iy[:, None] - 2)
    wz = spline_weight(jz[:, None] + 0.5 - 4 * iz[None, :] - 2)
    wxy = np.einsum("ij,de->idje", wx, wy).reshape(coarse_x * coarse_y, fine_x * fine_y)
    wxy = np.concatenate([wxy, wxy], axis=1).astype(np.float32)
    high = wxy.astype(BF16)
    low = (wxy - high.astype(np.float32)).astype(BF16)
    side = 8
    block = np.zeros((side, fine_z, side, coarse_z), np.float32)
    for i in range(side):
        block[i, :, i, :] = wz
    block = block.reshape(side * fine_z, side * coarse_z).astype(BF16)
    return np.concatenate([high, low], axis=0), block


def nt(a, b, precision=None):
    return lax.dot_general(
        a, b, (((1,), (1,)), ((), ())), precision=precision, preferred_element_type=F32
    )


def nn(a, b, precision=None):
    return jnp.dot(a, b, precision=precision, preferred_element_type=F32)


def from_row(x, i):
    return jnp.take_along_axis(x, jnp.full((8, LANES), i, jnp.int32), axis=0)


def eliminate(mats, width):
    sub = lax.broadcasted_iota(jnp.int32, (8, LANES), 0)
    for kb in range(0, RANK, width):
        v0, off = kb // 8, kb % 8
        for w in mats:
            cols = [
                [jnp.broadcast_to(w[v][:, kb + j : kb + j + 1], (8, LANES)) for v in range(8)]
                for j in range(width)
            ]
            r = [from_row(w[v0], off + i) for i in range(width)]
            e = [[from_row(cols[j][v0], off + i) for j in range(width)] for i in range(width)]
            for i in range(width):
                inv = 1.0 / e[i][i]
                r[i] = r[i] * inv
                for j in range(i + 1, width):
                    e[i][j] = e[i][j] * inv
                for k in range(width):
                    if k != i:
                        f = e[k][i]
                        r[k] = r[k] - f * r[i]
                        for j in range(i + 1, width):
                            e[k][j] = e[k][j] - f * e[i][j]
            for v in range(8):
                new = w[v]
                for j in range(width):
                    new = new - cols[j][v] * r[j]
                if v == v0:
                    for i in range(width):
                        new = jnp.where(sub == off + i, r[i], new)
                w[v] = new


def solve_all(mats, width=4):
    row = lax.broadcasted_iota(jnp.int32, (RANK, LANES), 0)
    lane = lax.broadcasted_iota(jnp.int32, (RANK, LANES), 1)
    diagonal = row == lane
    work = []
    for w in mats:
        trace = jnp.sum(jnp.where(diagonal, w, 0.0), axis=(0, 1), keepdims=True)
        ridge = 0.01 * trace / RANK + 1e-06
        w = jnp.where(diagonal, w + ridge, w)
        work.append([w[8 * v : 8 * v + 8] for v in range(8)])
    eliminate(work, width)
    out = []
    for w in work:
        full = jnp.concatenate(w, axis=0)
        full = full.astype(BF16).astype(F32)
        out.append(jnp.transpose(full)[RANK:])
    return out


def two_by_two(a, b, c, d):
    return jnp.concatenate(
        [jnp.concatenate([a, b], axis=1), jnp.concatenate([c, d], axis=1)], axis=0
    )


def kernel(
    scaling, shots, depth, owners,
    p_ref, s_ref, wxy_ref, wz_ref, sk_ref, pair_ref,
    out_ref,
    t_ref, own, hsend, hrecv, leaf, skt,
    m_ref, rs, red, zb, fin, ga, us, ur, u_ref,
    hs, hr, ys, yr, rss, rsr, zs, zr, gs, gr, uss, usr,
):
    group_at = pl.program_id(0)
    step = pl.program_id(1)
    chunk = p_ref.shape[1]
    last_step = pl.num_programs(1) - 1
    me = lax.axis_index("shots")
    sp = lax.axis_index("space")
    count = depth * owners
    z = sp // owners
    o = lax.rem(sp, owners)
    right = lax.rem(sp + 1, count)
    left = lax.rem(sp + count - 1, count)
    half = me // 2
    odd = lax.rem(me, 2)
    base = 4 * half
    group = 2 * owners
    line = odd * owners + o
    rows = LANES // owners
    twice = scaling * scaling

    def owner_peer(d):
        return (me, z * owners + lax.rem(o + d, owners))

    def depth_peer(d):
        return (me, lax.rem(z + d, depth) * owners + o)

    def shot_peer(d):
        return (lax.rem(me + d, shots), sp)

    def group_peer(d):
        peer = lax.rem(line + d, group)
        return (2 * half + peer // owners, z * owners + lax.rem(peer, owners))

    barrier = pltpu.get_barrier_semaphore()

    @pl.when(jnp.logical_and(group_at == 0, step == 0))
    def _():
        targets = [(me, left), (me, right)]
        targets += [depth_peer(d) for d in range(1, depth)]
        targets += [shot_peer(d) for d in range(1, shots)]
        targets += [group_peer(d) for d in range(1, group)]
        for target in targets:
            pl.semaphore_signal(barrier, inc=1, device_id=target, device_id_type=MESH)
        skt[...] = jnp.concatenate([sk_ref[x] for x in range(sk_ref.shape[0])], axis=1)

    def remote(src, dst, ssem, rsem, target):
        return pltpu.make_async_remote_copy(
            src_ref=src, dst_ref=dst, send_sem=ssem, recv_sem=rsem,
            device_id=target, device_id_type=MESH,
        )

    def halo_copies(g):
        return [
            remote(hsend.at[g, 0], hrecv.at[g, 0], hs.at[g, 0], hr.at[g, 0], (me, right)),
            remote(hsend.at[g, 1], hrecv.at[g, 1], hs.at[g, 1], hr.at[g, 1], (me, left)),
        ]

    def leaf_copies(g):
        mine = leaf.at[2 * me + g]
        return [
            remote(mine, mine, ys.at[g, d - 1], yr.at[g, d - 1], shot_peer(d))
            for d in range(1, shots)
        ]

    src = s_ref[0].reshape(256, LANES)
    wxy = wxy_ref[...]
    for a in range(0, chunk, 2):
        first = p_ref[0, a].reshape(256, LANES) * src
        other = p_ref[0, a + 1].reshape(256, LANES) * src
        both = nn(wxy, jnp.concatenate([first, other], axis=1))
        both = both[:16] + both[16:]
        row = pl.multiple_of((step * chunk + a) * 16, 32)
        t_ref[pl.ds(row, 16), :] = both[:, :LANES]
        t_ref[pl.ds(row + 16, 16), :] = both[:, LANES:]

    def finish_group(g):
        wz = wz_ref[...]
        for part in range(2):
            cols = [t_ref[pl.ds(part * 8 + k, RANK, stride=16), :] for k in range(8)]
            y = nn(jnp.concatenate([q.astype(BF16) for q in cols], axis=1), wz)
            if part == 0:
                hsend[g, 1] = y[:, :LANES].astype(BF16)
                own[g, :, :LANES] = y[:, LANES:]
            else:
                own[g, :, LANES:] = y[:, :LANES]
                hsend[g, 0] = y[:, LANES:].astype(BF16)

    def make_leaf(g):
        below = jnp.where(sp > 0, hrecv[g, 0].astype(F32), 0.0)
        above = jnp.where(sp < count - 1, hrecv[g, 1].astype(F32), 0.0)
        lead = (own[g, :, :LANES] + below).astype(BF16)
        tail = (own[g, :, LANES:] + above).astype(BF16)
        leaf[2 * me + g, :, :LANES] = lead
        leaf[2 * me + g, :, LANES:] = tail

    @pl.when(jnp.logical_and(group_at == 0, step == last_step))
    def _():
        finish_group(0)
        pl.semaphore_wait(barrier, 2 + depth - 1 + shots - 1 + group - 1)
        for c in halo_copies(0):
            c.start()

    @pl.when(jnp.logical_and(group_at == 1, step == last_step))
    def _():
        finish_group(1)
        for c in halo_copies(1):
            c.start()
        for c in halo_copies(0):
            c.wait()
        make_leaf(0)
        for c in leaf_copies(0):
            c.start()
        for c in halo_copies(1):
            c.wait()
        make_leaf(1)
        for c in leaf_copies(1):
            c.start()
        for g in range(2):
            for c in leaf_copies(g):
                c.wait()

        p0 = leaf[pair_ref[base + 2 * odd]]
        p1 = leaf[pair_ref[base + 2 * odd + 1]]
        sk = skt[...]

        def scatter(part):
            out = []
            for d in range(1, owners):
                peer = lax.rem(o + d, owners)
                src_rows = m_ref.at[part, pl.ds(pl.multiple_of(peer * rows, rows), rows)]
                out.append(
                    remote(
                        src_rows, rs.at[part, o], rss.at[part, d - 1], rsr.at[part, d - 1],
                        owner_peer(d),
                    )
                )
            for c in out:
                c.start()
            rs[part, o] = m_ref[part, pl.ds(pl.multiple_of(o * rows, rows), rows), :]
            return out

        def along(part, copies):
            for c in copies:
                c.wait()
            total = rs[part, 0]
            for k in range(1, owners):
                total = total + rs[part, k]
            red[part] = total
            out = [
                remote(
                    red.at[part], zb.at[part, z], zs.at[part, d - 1], zr.at[part, d - 1],
                    depth_peer(d),
                )
                for d in range(1, depth)
            ]
            for c in out:
                c.start()
            zb[part, z] = total
            return out

        def spread(part, copies):
            for c in copies:
                c.wait()
            total = zb[part, 0]
            for k in range(1, depth):
                total = total + zb[part, k]
            fin[part] = total
            out = [
                remote(
                    fin.at[part], ga.at[part, line], gs.at[part, d - 1], gr.at[part, d - 1],
                    group_peer(d),
                )
                for d in range(1, group)
            ]
            for c in out:
                c.start()
            ga[part, line] = total
            return out

        m_ref[0, 0:64, :] = nt(p0, jnp.concatenate([p0, sk], axis=0))
        m_ref[0, 64:128, :] = nt(p1, jnp.concatenate([p1, sk], axis=0))
        first = scatter(0)
        xx = leaf[pair_ref[base + 2 + odd]]
        q0 = leaf[pair_ref[base]]
        q1 = leaf[pair_ref[base + 1]]
        m_ref[1, 0:64, :] = nt(xx, jnp.concatenate([q0, q1], axis=0))
        m_ref[1, 64:128, :] = jnp.concatenate([nt(p0, p1), nt(p1, p0)], axis=1)
        other = scatter(1)
        first = along(0, first)
        other = along(1, other)
        first = spread(0, first)
        other = spread(1, other)
        for c in first:
            c.wait()
        per = RANK // rows

        def block(part, index):
            return jnp.concatenate([ga[part, index * per + k] for k in range(per)], axis=0)

        aug = [block(0, p) for p in range(4)]
        c = solve_all(aug)
        for cp in other:
            cp.wait()
        pair_cols, second_in = [], []
        for m in range(2):
            cc = jnp.concatenate([c[2 * m], c[2 * m + 1]], axis=1)
            a0, a1 = aug[2 * m], aug[2 * m + 1]
            mix = block(1, 2 * m + 1)
            h = two_by_two(a0[:, :RANK], mix[:, :RANK], mix[:, RANK:], a1[:, :RANK])
            x = jnp.concatenate([a0[:, RANK:], a1[:, RANK:]], axis=0)
            gm = nt(nt(cc, h, HI), cc, HI)
            xm = nn(cc, x, HI)
            second_in.append(jnp.concatenate([twice * gm, scaling * xm], axis=1))
            pair_cols.append(cc)
        k = jnp.concatenate([block(1, 0), block(1, 2)], axis=0)
        g01 = twice * nt(nt(pair_cols[0], k, HI), pair_cols[1], HI)
        g10 = twice * nt(nn(pair_cols[1], k, HI), pair_cols[0], HI)
        d = solve_all(second_in)
        dd = jnp.concatenate(d, axis=1)
        b0, b1 = second_in
        hm = two_by_two(b0[:, :RANK], g01, g10, b1[:, :RANK])
        x = jnp.concatenate([b0[:, RANK:], b1[:, RANK:]], axis=0)
        gm = nt(nt(dd, hm, HI), dd, HI)
        xm = nn(dd, x, HI)
        quad = twice * jnp.concatenate([nn(d[m], pair_cols[m], HI) for m in range(2)], axis=1)
        third = solve_all([jnp.concatenate([twice * gm, scaling * xm], axis=1)], 8)
        u_ref[...] = scaling * nn(third[0], quad, HI)
        width = out_ref.shape[1]
        partner = shots - 1 - me
        us[...] = u_ref[pl.ds(pl.multiple_of(partner * width, width), width), :].astype(BF16)
        trade = remote(us, ur, uss, usr, (partner, sp))
        trade.start()
        u = u_ref[pl.ds(pl.multiple_of(me * width, width), width), :].astype(BF16)
        total = None
        for p in range(4):
            term = nn(u[:, RANK * p : RANK * p + RANK], leaf[pair_ref[base + p]])
            total = term if total is None else total + term
        trade.wait()
        v = ur[...]
        for p in range(4):
            total = total + nn(v[:, RANK * p : RANK * p + RANK], leaf[pair_ref[4 - base + p]])
        for i in range(out_ref.shape[0]):
            out_ref[i] = total[:, RANK * i : RANK * i + RANK].astype(BF16)


def body(depth, probes, sources, sketch, pairing):
    groups, rank, steps, fine_x, fine_y, fine_z = probes.shape
    shots = lax.axis_size("shots")
    space = lax.axis_size("space")
    owners = space // depth
    wxy, wz = weight_tables(fine_x, fine_y, fine_z)
    fine_xy = fine_x * fine_y
    chunk = 16
    rows = LANES // owners
    group = 2 * owners
    dma = pltpu.SemaphoreType.DMA
    vmem = pltpu.VMEM
    scaling = math.sqrt(fine_x // 4 * space * 64 / rank)
    out_shape = (fine_x // 4, rank // shots, 64)
    return pl.pallas_call(
        functools.partial(kernel, scaling, shots, depth, owners),
        grid=(groups, rank // chunk),
        in_specs=[
            pl.BlockSpec((1, chunk, steps, fine_xy, fine_z), lambda g, a: (g, a, 0, 0, 0)),
            pl.BlockSpec((1, steps, fine_xy, fine_z), lambda g, a: (g, 0, 0, 0)),
            pl.BlockSpec(wxy.shape, lambda g, a: (0, 0)),
            pl.BlockSpec(wz.shape, lambda g, a: (0, 0)),
            pl.BlockSpec(sketch.shape, lambda g, a: (0, 0, 0)),
            pl.BlockSpec(memory_space=pltpu.SMEM),
        ],
        out_specs=pl.BlockSpec(out_shape, lambda g, a: (0, 0, 0)),
        out_shape=jax.ShapeDtypeStruct(out_shape, BF16),
        scratch_shapes=[
            vmem((rank * 16, LANES), F32),
            vmem((groups, rank, 256), F32),
            vmem((groups, 2, rank, LANES), BF16),
            vmem((groups, 2, rank, LANES), BF16),
            vmem((groups * shots, rank, 256), BF16),
            vmem((rank, 256), BF16),
            vmem((2, LANES, LANES), F32),
            vmem((2, owners, rows, LANES), F32),
            vmem((2, rows, LANES), F32),
            vmem((2, depth, rows, LANES), F32),
            vmem((2, rows, LANES), F32),
            vmem((2, group, rows, LANES), F32),
            vmem((rank // shots, 256), BF16),
            vmem((rank // shots, 256), BF16),
            vmem((rank, 256), F32),
            dma((groups, 2)), dma((groups, 2)),
            dma((groups, shots - 1)), dma((groups, shots - 1)),
            dma((2, owners - 1)), dma((2, owners - 1)),
            dma((2, depth - 1)), dma((2, depth - 1)),
            dma((2, group - 1)), dma((2, group - 1)),
            dma, dma,
        ],
        compiler_params=pltpu.CompilerParams(collective_id=0, has_side_effects=True),
        name="merge",
    )(
        probes.reshape(groups, rank, steps, fine_xy, fine_z),
        sources.reshape(groups, steps, fine_xy, fine_z),
        jnp.asarray(wxy),
        jnp.asarray(wz),
        sketch,
        pairing,
    )


def solution(mesh):
    in_specs = (
        P("shots", None, None, "space", None, None),
        P("shots", None, "space", None, None),
        P("space", None, None),
        P(),
    )
    out_specs = P("space", "shots", None)
    depth = 8 if mesh.shape["space"] == 64 else 2
    return jax.shard_map(
        functools.partial(body, depth),
        mesh=mesh, in_specs=in_specs, out_specs=out_specs, check_vma=False,
    )
```

time: 712 us -> 53.5 us (0.08)
  waiting for transfers between devices: 544 us -> 0 us
  other arithmetic: 85.6 us -> 0 us
  Pallas kernels: 0 us -> 51.9 us
  matrix products: 44.5 us -> 0 us
  between operations: 13.4 us -> 0.01 us
  starting transfers between devices: 11.2 us -> 0 us
  blocking collectives: 11.1 us -> 0 us
    psum x3 -> x0, waiting for transfers between devices: 533 us -> none  [merge_level(): gram_mats, cross_mats = lax.psum((gram_mats, cross_mats), 'space')]
    another operation x19 -> x0, other arithmetic: 65.5 us -> none  [the longest x10 35.6 us: solve_coef(): jnp.linalg.cholesky(gram_mats + ridge_term[:, None, None] * identity)]
    pallas_call x0 -> x1, Pallas kernels: none -> 51.9 us  [body(): pl.pallas_call(functools.partial(kernel, scaling, shots, depth, owners),...]
    dot_general x12 -> x0, matrix products: 40.5 us -> none  [the longest x1 28.1 us: body(): jnp.einsum('gaxyz,zc->gaxyc', images, spline_table(fine_z, coarse_z, 0, 0...]
    ppermute x4 -> x0, starting transfers between devices: 11.1 us -> none  [the longest x1 5.11 us: extended(): after = lax.ppermute(initial, axis, down)]
    all_gather x1 -> x0, blocking collectives: 11.1 us -> none  [body(): gathered = lax.all_gather(leaves, 'shots', axis=0, tiled=True)]
    unnamed x2 -> x0, other arithmetic: 10.9 us -> none
    ppermute x4 -> x0, waiting for transfers between devices: 10.2 us -> none  [the longest x2 4.33 us: from_partner(): return lax.ppermute(value, axis, pairs)]
  transfers between devices with their start and end apart: 7 -> 0, of which waited for: 7 -> 0; matrix products, arithmetic and copies ran while one was open for 0% -> 0% of each run, Pallas kernels for 0% -> 0%
where the time goes in v2:
time: 53.5 us; the launch traced here: 53.2 us
  Pallas kernels  51.9 us (97%)
  local copies, waits for them, and re-layouts  1.32 us (2%)
    pallas_call x1, Pallas kernels, body(): pl.pallas_call(functools.partial(kernel, scaling, shots, depth, owners),...  51.9 us
    unnamed x1, local copies, waits for them, and re-layouts  1.32 us

profile of v2, /device:TPU:1, one launch (start us, length us, event | category | flops | bytes accessed | tf_op | source)
XLA Modules:
  0.0 53.2 jit_solution(2312344237779333314)
XLA Ops:
  0.0 51.9 %merge.1 = bf16[4,16,64]{2,1,0:T(8,128)(2,1)} custom-call(bf16[2,64,2,128,128]{4,3,2,1,0:T(8,128)(2,1)} %bitcast.2, bf16[2,2,128,128]{3,2,1,0:T(8,128)(2,1)} %bitcast.3, bf16[32,256]{1,0:T(8,128)(2,1)} %constant.4.clone.wxy_ref, bf16[1024,256]{1,0:T(8,128)(2,1)} %constant.5.clone.wz_ref, bf16[4,64,64]{2,1,0:T(8,128)(2,1)} %sk_ref.1, s32[8]{0:T(128)} %pair_ref.1), custom_call_target="tpu_custom_call" | custom-call | tf_op jit(solution)/shard_map/merge/pallas_call | solution.py:383
  51.9 1.3 %copy.8 = bf16[4,16,64]{2,1,0:T(8,128)(2,1)} copy(bf16[4,16,64]{2,1,0:T(8,128)(2,1)} %merge.1) | data formatting | bytes 16384

commit v3 on v2

v3 whole, which is shorter than its diff:
```python
import functools
import math

import jax
import jax.numpy as jnp
import numpy as np
from jax import lax
from jax.experimental import pallas as pl
from jax.experimental.pallas import tpu as pltpu
from jax.sharding import PartitionSpec as P

MESH = pl.DeviceIdType.MESH
F32 = jnp.float32
BF16 = jnp.bfloat16
RANK = 64
LANES = 128


def spline_weight(distance):
    s = np.abs(distance / 4.0)
    inner = 2.0 / 3.0 - s**2 + 0.5 * s**3
    outer = np.maximum(2.0 - s, 0.0) ** 3 / 6.0
    return np.where(s < 1.0, inner, outer) / 4.0


def weight_tables(fine_x, fine_y, fine_z):
    coarse_x, coarse_y, coarse_z = fine_x // 4 + 4, fine_y // 4, fine_z // 4
    jx, jy, jz = np.arange(fine_x), np.arange(fine_y), np.arange(fine_z)
    ix, iy, iz = np.arange(coarse_x) - 2, np.arange(coarse_y), np.arange(coarse_z)
    wx = spline_weight(jx[None, :] + 0.5 - 4 * ix[:, None] - 2)
    wy = spline_weight(jy[None, :] + 0.5 - 4 * iy[:, None] - 2)
    wz = spline_weight(jz[:, None] + 0.5 - 4 * iz[None, :] - 2)
    wxy = np.einsum("ij,de->idje", wx, wy).reshape(coarse_x * coarse_y, fine_x * fine_y)
    wxy = np.concatenate([wxy, wxy], axis=1).astype(np.float32)
    high = wxy.astype(BF16)
    low = (wxy - high.astype(np.float32)).astype(BF16)
    side = 8
    block = np.zeros((side, fine_z, side, coarse_z), np.float32)
    for i in range(side):
        block[i, :, i, :] = wz
    block = block.reshape(side * fine_z, side * coarse_z).astype(BF16)
    return np.concatenate([high, low], axis=0), block


def nt(a, b):
    return lax.dot_general(
        a, b, (((1,), (1,)), ((), ())), preferred_element_type=F32
    )


def nn(a, b):
    return jnp.dot(a, b, preferred_element_type=F32)


def from_row(x, i):
    return jnp.take_along_axis(x, jnp.full((8, LANES), i, jnp.int32), axis=0)


def eliminate(mats, width):
    sub = lax.broadcasted_iota(jnp.int32, (8, LANES), 0)
    for kb in range(0, RANK, width):
        v0, off = kb // 8, kb % 8
        for w in mats:
            cols = [
                [jnp.broadcast_to(w[v][:, kb + j : kb + j + 1], (8, LANES)) for v in range(8)]
                for j in range(width)
            ]
            r = [from_row(w[v0], off + i) for i in range(width)]
            e = [[from_row(cols[j][v0], off + i) for j in range(width)] for i in range(width)]
            for i in range(width):
                inv = 1.0 / e[i][i]
                r[i] = r[i] * inv
                for j in range(i + 1, width):
                    e[i][j] = e[i][j] * inv
                for k in range(width):
                    if k != i:
                        f = e[k][i]
                        r[k] = r[k] - f * r[i]
                        for j in range(i + 1, width):
                            e[k][j] = e[k][j] - f * e[i][j]
            for v in range(8):
                new = w[v]
                for j in range(width):
                    new = new - cols[j][v] * r[j]
                if v == v0:
                    for i in range(width):
                        new = jnp.where(sub == off + i, r[i], new)
                w[v] = new


def solve_all(mats, width=4):
    row = lax.broadcasted_iota(jnp.int32, (RANK, LANES), 0)
    lane = lax.broadcasted_iota(jnp.int32, (RANK, LANES), 1)
    diagonal = row == lane
    work = []
    for w in mats:
        trace = jnp.sum(jnp.where(diagonal, w, 0.0), axis=(0, 1), keepdims=True)
        ridge = 0.01 * trace / RANK + 1e-06
        w = jnp.where(diagonal, w + ridge, w)
        work.append([w[8 * v : 8 * v + 8] for v in range(8)])
    eliminate(work, width)
    out = []
    for w in work:
        full = jnp.concatenate(w, axis=0)
        out.append(jnp.transpose(full)[RANK:].astype(BF16))
    return out


def split(x, terms):
    out = []
    for _ in range(terms - 1):
        part = x.astype(BF16)
        out.append(part)
        x = x - part.astype(F32)
    out.append(x.astype(BF16))
    return out


def exact_nn(c, x, terms=3):
    return nn(jnp.concatenate([c] * terms, axis=1), jnp.concatenate(split(x, terms), axis=0))


def exact_nt(x, c, terms=3):
    return nt(jnp.concatenate(split(x, terms), axis=1), jnp.concatenate([c] * terms, axis=1))


def gram_and_cross(c, h, x, scaling):
    both = exact_nn(c, jnp.concatenate([h, x], axis=1))
    gm = exact_nt(both[:, :LANES], c)
    return jnp.concatenate([(scaling * scaling) * gm, scaling * both[:, LANES:]], axis=1)


def two_by_two(a, b, c, d):
    return jnp.concatenate(
        [jnp.concatenate([a, b], axis=1), jnp.concatenate([c, d], axis=1)], axis=0
    )


def kernel(
    scaling, shots, depth, owners,
    p_hbm, s_hbm, wxy_hbm, wz_hbm, sk_hbm, pair_ref,
    out_ref,
    p_ref, s_ref, wxy_ref, wz_ref, sk_ref, psem, csem,
    t_ref, own, hsend, hrecv, leaf, skt,
    m_ref, rs, red, zb, fin, ga, us, ur, u_ref,
    hs, hr, ys, yr, rss, rsr, zs, zr, gs, gr, uss, usr,
):
    chunk = 16
    blocks = RANK // chunk

    def load(g, i):
        at = pl.ds(i * chunk, chunk)
        return pltpu.make_async_copy(p_hbm.at[g, at], p_ref.at[g, at], psem.at[g, i])

    small = [
        pltpu.make_async_copy(src, dst, csem.at[i])
        for i, (src, dst) in enumerate(
            [(s_hbm, s_ref), (wxy_hbm, wxy_ref), (wz_hbm, wz_ref), (sk_hbm, sk_ref)]
        )
    ]
    small[0].start()
    small[1].start()
    for i in range(blocks):
        load(0, i).start()
    small[2].start()
    for i in range(blocks):
        load(1, i).start()
    small[3].start()
    me = lax.axis_index("shots")
    sp = lax.axis_index("space")
    count = depth * owners
    z = sp // owners
    o = lax.rem(sp, owners)
    right = lax.rem(sp + 1, count)
    left = lax.rem(sp + count - 1, count)
    half = me // 2
    odd = lax.rem(me, 2)
    base = 4 * half
    group = 2 * owners
    line = odd * owners + o
    rows = LANES // owners
    twice = scaling * scaling

    def owner_peer(d):
        return (me, z * owners + lax.rem(o + d, owners))

    def depth_peer(d):
        return (me, lax.rem(z + d, depth) * owners + o)

    def shot_peer(d):
        return (lax.rem(me + d, shots), sp)

    def group_peer(d):
        peer = lax.rem(line + d, group)
        return (2 * half + peer // owners, z * owners + lax.rem(peer, owners))

    barrier = pltpu.get_barrier_semaphore()

    targets = [(me, left), (me, right)]
    targets += [depth_peer(d) for d in range(1, depth)]
    targets += [shot_peer(d) for d in range(1, shots)]
    targets += [group_peer(d) for d in range(1, group)]
    for target in targets:
        pl.semaphore_signal(barrier, inc=1, device_id=target, device_id_type=MESH)

    def remote(src, dst, ssem, rsem, target):
        return pltpu.make_async_remote_copy(
            src_ref=src, dst_ref=dst, send_sem=ssem, recv_sem=rsem,
            device_id=target, device_id_type=MESH,
        )

    def halo_copies(g):
        return [
            remote(hsend.at[g, 0], hrecv.at[g, 0], hs.at[g, 0], hr.at[g, 0], (me, right)),
            remote(hsend.at[g, 1], hrecv.at[g, 1], hs.at[g, 1], hr.at[g, 1], (me, left)),
        ]

    def leaf_copies(g):
        mine = leaf.at[2 * me + g]
        return [
            remote(mine, mine, ys.at[g, d - 1], yr.at[g, d - 1], shot_peer(d))
            for d in range(1, shots)
        ]

    small[0].wait()
    small[1].wait()
    wxy = wxy_ref[...]

    def restrict_group(g):
        src = s_ref[g].reshape(256, LANES)

        def one(i, carry):
            load(g, i).wait()
            for a in range(0, chunk, 2):
                at = i * chunk + a
                first = p_ref[g, at].reshape(256, LANES) * src
                other = p_ref[g, at + 1].reshape(256, LANES) * src
                both = nn(wxy, jnp.concatenate([first, other], axis=1))
                both = both[:16] + both[16:]
                row = pl.multiple_of(at * 16, 32)
                t_ref[pl.ds(row, 16), :] = both[:, :LANES]
                t_ref[pl.ds(row + 16, 16), :] = both[:, LANES:]
            return carry

        lax.fori_loop(0, blocks, one, 0)

    def finish_group(g):
        wz = wz_ref[...]
        for part in range(2):
            cols = [t_ref[pl.ds(part * 8 + k, RANK, stride=16), :] for k in range(8)]
            y = nn(jnp.concatenate([q.astype(BF16) for q in cols], axis=1), wz)
            if part == 0:
                hsend[g, 1] = y[:, :LANES].astype(BF16)
                own[g, :, :LANES] = y[:, LANES:]
            else:
                own[g, :, LANES:] = y[:, :LANES]
                hsend[g, 0] = y[:, LANES:].astype(BF16)

    def make_leaf(g):
        below = jnp.where(sp > 0, hrecv[g, 0].astype(F32), 0.0)
        above = jnp.where(sp < count - 1, hrecv[g, 1].astype(F32), 0.0)
        lead = (own[g, :, :LANES] + below).astype(BF16)
        tail = (own[g, :, LANES:] + above).astype(BF16)
        leaf[2 * me + g, :, :LANES] = lead
        leaf[2 * me + g, :, LANES:] = tail

    restrict_group(0)
    small[2].wait()
    finish_group(0)
    pl.semaphore_wait(barrier, len(targets))
    for c in halo_copies(0):
        c.start()
    restrict_group(1)
    finish_group(1)
    for c in halo_copies(1):
        c.start()
    small[3].wait()
    skt[...] = jnp.concatenate([sk_ref[x] for x in range(sk_ref.shape[0])], axis=1)
    for c in halo_copies(0):
        c.wait()
    make_leaf(0)
    for c in leaf_copies(0):
        c.start()
    for c in halo_copies(1):
        c.wait()
    make_leaf(1)
    for c in leaf_copies(1):
        c.start()
    for g in range(2):
        for c in leaf_copies(g):
            c.wait()

    p0 = leaf[pair_ref[base + 2 * odd]]
    p1 = leaf[pair_ref[base + 2 * odd + 1]]
    sk = skt[...]

    def scatter(part):
        out = []
        for d in range(1, owners):
            peer = lax.rem(o + d, owners)
            src_rows = m_ref.at[part, pl.ds(pl.multiple_of(peer * rows, rows), rows)]
            out.append(
                remote(
                    src_rows, rs.at[part, o], rss.at[part, d - 1], rsr.at[part, d - 1],
                    owner_peer(d),
                )
            )
        for c in out:
            c.start()
        rs[part, o] = m_ref[part, pl.ds(pl.multiple_of(o * rows, rows), rows), :]
        return out

    def along(part, copies):
        for c in copies:
            c.wait()
        total = rs[part, 0]
        for k in range(1, owners):
            total = total + rs[part, k]
        red[part] = total
        out = [
            remote(
                red.at[part], zb.at[part, z], zs.at[part, d - 1], zr.at[part, d - 1],
                depth_peer(d),
            )
            for d in range(1, depth)
        ]
        for c in out:
            c.start()
        zb[part, z] = total
        return out

    def spread(part, copies):
        for c in copies:
            c.wait()
        total = zb[part, 0]
        for k in range(1, depth):
            total = total + zb[part, k]
        fin[part] = total
        out = [
            remote(
                fin.at[part], ga.at[part, line], gs.at[part, d - 1], gr.at[part, d - 1],
                group_peer(d),
            )
            for d in range(1, group)
        ]
        for c in out:
            c.start()
        ga[part, line] = total
        return out

    m_ref[0, 0:64, :] = nt(p0, jnp.concatenate([p0, sk], axis=0))
    m_ref[0, 64:128, :] = nt(p1, jnp.concatenate([p1, sk], axis=0))
    first = scatter(0)
    xx = leaf[pair_ref[base + 2 + odd]]
    q0 = leaf[pair_ref[base]]
    q1 = leaf[pair_ref[base + 1]]
    m_ref[1, 0:64, :] = nt(xx, jnp.concatenate([q0, q1], axis=0))
    m_ref[1, 64:128, :] = jnp.concatenate([nt(p0, p1), nt(p1, p0)], axis=1)
    other = scatter(1)
    first = along(0, first)
    other = along(1, other)
    first = spread(0, first)
    other = spread(1, other)
    for c in first:
        c.wait()
    per = RANK // rows

    def block(part, index):
        return jnp.concatenate([ga[part, index * per + k] for k in range(per)], axis=0)

    aug = [block(0, p) for p in range(4)]
    c = solve_all(aug)
    for cp in other:
        cp.wait()
    pair_cols, second_in = [], []
    for m in range(2):
        cc = jnp.concatenate([c[2 * m], c[2 * m + 1]], axis=1)
        a0, a1 = aug[2 * m], aug[2 * m + 1]
        mix = block(1, 2 * m + 1)
        h = two_by_two(a0[:, :RANK], mix[:, :RANK], mix[:, RANK:], a1[:, :RANK])
        x = jnp.concatenate([a0[:, RANK:], a1[:, RANK:]], axis=0)
        second_in.append(gram_and_cross(cc, h, x, scaling))
        pair_cols.append(cc)
    k = jnp.concatenate([block(1, 0), block(1, 2)], axis=0)
    g10 = twice * exact_nt(exact_nn(pair_cols[1], k), pair_cols[0])
    g01 = jnp.transpose(g10)
    d = solve_all(second_in)
    dd = jnp.concatenate(d, axis=1)
    b0, b1 = second_in
    hm = two_by_two(b0[:, :RANK], g01, g10, b1[:, :RANK])
    x = jnp.concatenate([b0[:, RANK:], b1[:, RANK:]], axis=0)
    quad = twice * jnp.concatenate([nn(d[m], pair_cols[m]) for m in range(2)], axis=1)
    third = solve_all([gram_and_cross(dd, hm, x, scaling)], 8)
    u_ref[...] = scaling * exact_nn(third[0], quad, 2)
    width = out_ref.shape[1]
    partner = shots - 1 - me
    us[...] = u_ref[pl.ds(pl.multiple_of(partner * width, width), width), :].astype(BF16)
    trade = remote(us, ur, uss, usr, (partner, sp))
    trade.start()
    u = u_ref[pl.ds(pl.multiple_of(me * width, width), width), :].astype(BF16)
    total = None
    for p in range(4):
        term = nn(u[:, RANK * p : RANK * p + RANK], leaf[pair_ref[base + p]])
        total = term if total is None else total + term
    trade.wait()
    v = ur[...]
    for p in range(4):
        total = total + nn(v[:, RANK * p : RANK * p + RANK], leaf[pair_ref[4 - base + p]])
    for i in range(out_ref.shape[0]):
        out_ref[i] = total[:, RANK * i : RANK * i + RANK].astype(BF16)


def body(depth, probes, sources, sketch, pairing):
    groups, rank, steps, fine_x, fine_y, fine_z = probes.shape
    shots = lax.axis_size("shots")
    space = lax.axis_size("space")
    owners = space // depth
    wxy, wz = weight_tables(fine_x, fine_y, fine_z)
    fine_xy = fine_x * fine_y
    chunk = 16
    rows = LANES // owners
    group = 2 * owners
    dma = pltpu.SemaphoreType.DMA
    vmem = pltpu.VMEM
    scaling = math.sqrt(fine_x // 4 * space * 64 / rank)
    out_shape = (fine_x // 4, rank // shots, 64)
    return pl.pallas_call(
        functools.partial(kernel, scaling, shots, depth, owners),
        in_specs=[pl.BlockSpec(memory_space=pl.ANY)] * 5
        + [pl.BlockSpec(memory_space=pltpu.SMEM)],
        out_specs=pl.BlockSpec(memory_space=pltpu.VMEM),
        out_shape=jax.ShapeDtypeStruct(out_shape, BF16),
        scratch_shapes=[
            vmem((groups, rank, steps, fine_xy, fine_z), BF16),
            vmem((groups, steps, fine_xy, fine_z), BF16),
            vmem(wxy.shape, BF16),
            vmem(wz.shape, BF16),
            vmem(sketch.shape, BF16),
            dma((groups, rank // chunk)),
            dma((4,)),
            vmem((rank * 16, LANES), F32),
            vmem((groups, rank, 256), F32),
            vmem((groups, 2, rank, LANES), BF16),
            vmem((groups, 2, rank, LANES), BF16),
            vmem((groups * shots, rank, 256), BF16),
            vmem((rank, 256), BF16),
            vmem((2, LANES, LANES), F32),
            vmem((2, owners, rows, LANES), F32),
            vmem((2, rows, LANES), F32),
            vmem((2, depth, rows, LANES), F32),
            vmem((2, rows, LANES), F32),
            vmem((2, group, rows, LANES), F32),
            vmem((rank // shots, 256), BF16),
            vmem((rank // shots, 256), BF16),
            vmem((rank, 256), F32),
            dma((groups, 2)), dma((groups, 2)),
            dma((groups, shots - 1)), dma((groups, shots - 1)),
            dma((2, owners - 1)), dma((2, owners - 1)),
            dma((2, depth - 1)), dma((2, depth - 1)),
            dma((2, group - 1)), dma((2, group - 1)),
            dma, dma,
        ],
        compiler_params=pltpu.CompilerParams(collective_id=0, has_side_effects=True),
        name="merge",
    )(
        probes.reshape(groups, rank, steps, fine_xy, fine_z),
        sources.reshape(groups, steps, fine_xy, fine_z),
        jnp.asarray(wxy),
        jnp.asarray(wz),
        sketch,
        pairing,
    )


def solution(mesh):
    in_specs = (
        P("shots", None, None, "space", None, None),
        P("shots", None, "space", None, None),
        P("space", None, None),
        P(),
    )
    out_specs = P("space", "shots", None)
    depth = 8 if mesh.shape["space"] == 64 else 2
    return jax.shard_map(
        functools.partial(body, depth),
        mesh=mesh, in_specs=in_specs, out_specs=out_specs, check_vma=False,
    )
```

time: 53.5 us -> 49.6 us (0.927)
  Pallas kernels: 51.9 us -> 48 us
    pallas_call x1, Pallas kernels: 51.9 us -> 48 us  [body(): pl.pallas_call(functools.partial(kernel, scaling, shots, depth, owners),...]
where the time goes in v3:
time: 49.6 us; the launch traced here: 49.4 us
  Pallas kernels  48 us (97%)
  local copies, waits for them, and re-layouts  1.32 us (3%)
    pallas_call x1, Pallas kernels, body(): pl.pallas_call(functools.partial(kernel, scaling, shots, depth, owners),...  48 us
    unnamed x1, local copies, waits for them, and re-layouts  1.32 us

profile of v3, /device:TPU:1, one launch (start us, length us, event | category | flops | bytes accessed | tf_op | source)
XLA Modules:
  0.0 49.4 jit_solution(2049070181253669902)
XLA Ops:
  0.0 48.0 %merge.1 = bf16[4,16,64]{2,1,0:T(8,128)(2,1)} custom-call(bf16[2,64,2,128,128]{4,3,2,1,0:T(8,128)(2,1)} %bitcast.2, bf16[2,2,128,128]{3,2,1,0:T(8,128)(2,1)} %bitcast.3, bf16[32,256]{1,0:T(8,128)(2,1)} %constant.4.clone.wxy_hbm, bf16[1024,256]{1,0:T(8,128)(2,1)} %constant.5.clone.wz_hbm, bf16[4,64,64]{2,1,0:T(8,128)(2,1)} %sk_hbm.1, s32[8]{0:T(128)} %pair_ref.1), custom_call_target="tpu_custom_call" | custom-call | tf_op jit(solution)/shard_map/merge/pallas_call | solution.py:427
  48.1 1.3 %copy.8 = bf16[4,16,64]{2,1,0:T(8,128)(2,1)} copy(bf16[4,16,64]{2,1,0:T(8,128)(2,1)} %merge.1) | data formatting | bytes 16384

commit v4 on v3

--- a/solution.py
+++ b/solution.py
@@ -141,7 +141,7 @@
     p_hbm, s_hbm, wxy_hbm, wz_hbm, sk_hbm, pair_ref,
     out_ref,
     p_ref, s_ref, wxy_ref, wz_ref, sk_ref, psem, csem,
-    t_ref, own, hsend, hrecv, leaf, skt,
+    t_ref, part_of, hsend, hrecv, leaf, skt,
     m_ref, rs, red, zb, fin, ga, us, ur, u_ref,
     hs, hr, ys, yr, rss, rsr, zs, zr, gs, gr, uss, usr,
 ):
@@ -181,8 +181,27 @@
     rows = LANES // owners
     twice = scaling * scaling
 
-    def owner_peer(d):
-        return (me, z * owners + lax.rem(o + d, owners))
+    across = owners // 2
+    at_x = o // 2
+    core = lax.rem(o, 2)
+
+    def ring(d, size):
+        return min(d, size - d)
+
+    def near(dx, dc):
+        return lax.rem(at_x + dx, across) * 2 + lax.rem(core + dc, 2)
+
+    group_offsets = sorted(
+        [(dy, dx, dc) for dy in range(2) for dx in range(across) for dc in range(2)][1:],
+        key=lambda d: (-d[0] - ring(d[1], across), -d[2]),
+    )
+    owner_offsets = [d for d in group_offsets if d[0] == 0]
+    depth_offsets = sorted(range(1, depth), key=lambda d: -ring(d, depth))
+    shot_offsets = sorted(range(shots), key=lambda d: -ring(d, shots))
+
+    def slot(offset):
+        dy, dx, dc = offset
+        return dy * owners + dx * 2 + dc - 1
 
     def depth_peer(d):
         return (me, lax.rem(z + d, depth) * owners + o)
@@ -190,16 +209,16 @@
     def shot_peer(d):
         return (lax.rem(me + d, shots), sp)
 
-    def group_peer(d):
-        peer = lax.rem(line + d, group)
-        return (2 * half + peer // owners, z * owners + lax.rem(peer, owners))
+    def group_peer(offset):
+        dy, dx, dc = offset
+        return (2 * half + lax.rem(odd + dy, 2), z * owners + near(dx, dc))
 
     barrier = pltpu.get_barrier_semaphore()
 
-    targets = [(me, left), (me, right)]
-    targets += [depth_peer(d) for d in range(1, depth)]
-    targets += [shot_peer(d) for d in range(1, shots)]
-    targets += [group_peer(d) for d in range(1, group)]
+    targets = [(lax.rem(me + d, shots), side) for d in shot_offsets for side in (left, right)]
+    targets += [depth_peer(d) for d in depth_offsets]
+    targets += [shot_peer(d) for d in shot_offsets if d]
+    targets += [group_peer(d) for d in group_offsets]
     for target in targets:
         pl.semaphore_signal(barrier, inc=1, device_id=target, device_id_type=MESH)
 
@@ -209,18 +228,21 @@
             device_id=target, device_id_type=MESH,
         )
 
-    def halo_copies(g):
-        return [
-            remote(hsend.at[g, 0], hrecv.at[g, 0], hs.at[g, 0], hr.at[g, 0], (me, right)),
-            remote(hsend.at[g, 1], hrecv.at[g, 1], hs.at[g, 1], hr.at[g, 1], (me, left)),
-        ]
-
-    def leaf_copies(g):
-        mine = leaf.at[2 * me + g]
-        return [
-            remote(mine, mine, ys.at[g, d - 1], yr.at[g, d - 1], shot_peer(d))
-            for d in range(1, shots)
-        ]
+    def piece_copies(g):
+        mine = part_of.at[2 * me + g]
+        out = []
+        for d in shot_offsets:
+            shot = lax.rem(me + d, shots)
+            for side, peer in enumerate((right, left)):
+                out.append(
+                    remote(
+                        hsend.at[g, side], hrecv.at[2 * me + g, side],
+                        hs.at[g, side, d], hr.at[g, side, d], (shot, peer),
+                    )
+                )
+            if d:
+                out.append(remote(mine, mine, ys.at[g, d - 1], yr.at[g, d - 1], (shot, sp)))
+        return out
 
     small[0].wait()
     small[1].wait()
@@ -251,44 +273,35 @@
             y = nn(jnp.concatenate([q.astype(BF16) for q in cols], axis=1), wz)
             if part == 0:
                 hsend[g, 1] = y[:, :LANES].astype(BF16)
-                own[g, :, :LANES] = y[:, LANES:]
+                part_of[2 * me + g, :, :LANES] = y[:, LANES:].astype(BF16)
             else:
-                own[g, :, LANES:] = y[:, :LANES]
+                part_of[2 * me + g, :, LANES:] = y[:, :LANES].astype(BF16)
                 hsend[g, 0] = y[:, LANES:].astype(BF16)
 
-    def make_leaf(g):
-        below = jnp.where(sp > 0, hrecv[g, 0].astype(F32), 0.0)
-        above = jnp.where(sp < count - 1, hrecv[g, 1].astype(F32), 0.0)
-        lead = (own[g, :, :LANES] + below).astype(BF16)
-        tail = (own[g, :, LANES:] + above).astype(BF16)
-        leaf[2 * me + g, :, :LANES] = lead
-        leaf[2 * me + g, :, LANES:] = tail
+    def make_leaf(q):
+        below = jnp.where(sp > 0, hrecv[q, 0].astype(F32), 0.0)
+        above = jnp.where(sp < count - 1, hrecv[q, 1].astype(F32), 0.0)
+        leaf[q, :, :LANES] = (part_of[q, :, :LANES].astype(F32) + below).astype(BF16)
+        leaf[q, :, LANES:] = (part_of[q, :, LANES:].astype(F32) + above).astype(BF16)
 
     restrict_group(0)
     small[2].wait()
     finish_group(0)
     pl.semaphore_wait(barrier, len(targets))
-    for c in halo_copies(0):
+    early = piece_copies(0)
+    for c in early:
         c.start()
     restrict_group(1)
     finish_group(1)
-    for c in halo_copies(1):
+    late = piece_copies(1)
+    for c in late:
         c.start()
     small[3].wait()
     skt[...] = jnp.concatenate([sk_ref[x] for x in range(sk_ref.shape[0])], axis=1)
-    for c in halo_copies(0):
+    for c in early + late:
         c.wait()
-    make_leaf(0)
-    for c in leaf_copies(0):
-        c.start()
-    for c in halo_copies(1):
-        c.wait()
-    make_leaf(1)
-    for c in leaf_copies(1):
-        c.start()
-    for g in range(2):
-        for c in leaf_copies(g):
-            c.wait()
+    for q in range(2 * shots):
+        make_leaf(q)
 
     p0 = leaf[pair_ref[base + 2 * odd]]
     p1 = leaf[pair_ref[base + 2 * odd + 1]]
@@ -296,13 +309,13 @@
 
     def scatter(part):
         out = []
-        for d in range(1, owners):
-            peer = lax.rem(o + d, owners)
+        for d in owner_offsets:
+            peer = near(d[1], d[2])
             src_rows = m_ref.at[part, pl.ds(pl.multiple_of(peer * rows, rows), rows)]
             out.append(
                 remote(
-                    src_rows, rs.at[part, o], rss.at[part, d - 1], rsr.at[part, d - 1],
-                    owner_peer(d),
+                    src_rows, rs.at[part, o], rss.at[part, slot(d)], rsr.at[part, slot(d)],
+                    group_peer(d),
                 )
             )
         for c in out:
@@ -322,7 +335,7 @@
                 red.at[part], zb.at[part, z], zs.at[part, d - 1], zr.at[part, d - 1],
                 depth_peer(d),
             )
-            for d in range(1, depth)
+            for d in depth_offsets
         ]
         for c in out:
             c.start()
@@ -338,10 +351,10 @@
         fin[part] = total
         out = [
             remote(
-                fin.at[part], ga.at[part, line], gs.at[part, d - 1], gr.at[part, d - 1],
+                fin.at[part], ga.at[part, line], gs.at[part, slot(d)], gr.at[part, slot(d)],
                 group_peer(d),
             )
-            for d in range(1, group)
+            for d in group_offsets
         ]
         for c in out:
             c.start()
@@ -429,7 +442,7 @@
         in_specs=[pl.BlockSpec(memory_space=pl.ANY)] * 5
         + [pl.BlockSpec(memory_space=pltpu.SMEM)],
         out_specs=pl.BlockSpec(memory_space=pltpu.VMEM),
-        out_shape=jax.ShapeDtypeStruct(out_shape, BF16),
+        out_shape=pltpu.VMEM(out_shape, BF16),
         scratch_shapes=[
             vmem((groups, rank, steps, fine_xy, fine_z), BF16),
             vmem((groups, steps, fine_xy, fine_z), BF16),
@@ -439,9 +452,9 @@
             dma((groups, rank // chunk)),
             dma((4,)),
             vmem((rank * 16, LANES), F32),
-            vmem((groups, rank, 256), F32),
+            vmem((groups * shots, rank, 256), BF16),
             vmem((groups, 2, rank, LANES), BF16),
-            vmem((groups, 2, rank, LANES), BF16),
+            vmem((groups * shots, 2, rank, LANES), BF16),
             vmem((groups * shots, rank, 256), BF16),
             vmem((rank, 256), BF16),
             vmem((2, LANES, LANES), F32),
@@ -453,7 +466,7 @@
             vmem((rank // shots, 256), BF16),
             vmem((rank // shots, 256), BF16),
             vmem((rank, 256), F32),
-            dma((groups, 2)), dma((groups, 2)),
+            dma((groups, 2, shots)), dma((groups, 2, shots)),
             dma((groups, shots - 1)), dma((groups, shots - 1)),
             dma((2, owners - 1)), dma((2, owners - 1)),
             dma((2, depth - 1)), dma((2, depth - 1)),

time: 49.6 us -> 46.8 us (0.944)
  Pallas kernels: 48 us -> 46.1 us
  local copies, waits for them, and re-layouts: 1.32 us -> 0.61 us
    pallas_call x1, Pallas kernels: 48 us -> 46.1 us  [body(): pl.pallas_call(functools.partial(kernel, scaling, shots, depth, owners),...]
    unnamed x1, local copies, waits for them, and re-layouts: 1.32 us -> 0.61 us
where the time goes in v4:
time: 46.8 us; the launch traced here: 46.7 us
  Pallas kernels  46.1 us (99%)
  local copies, waits for them, and re-layouts  0.61 us (1%)
    pallas_call x1, Pallas kernels, body(): pl.pallas_call(functools.partial(kernel, scaling, shots, depth, owners),...  46.1 us

profile of v4, /device:TPU:1, one launch (start us, length us, event | category | flops | bytes accessed | tf_op | source)
XLA Modules:
  0.0 46.7 jit_solution(12553009074360441801)
XLA Ops:
  0.0 46.1 %merge.1 = bf16[4,16,64]{2,1,0:T(8,128)(2,1)S(1)} custom-call(bf16[2,64,2,128,128]{4,3,2,1,0:T(8,128)(2,1)} %bitcast.2, bf16[2,2,128,128]{3,2,1,0:T(8,128)(2,1)} %bitcast.3, bf16[32,256]{1,0:T(8,128)(2,1)} %constant.4.clone.wxy_hbm, bf16[1024,256]{1,0:T(8,128)(2,1)} %constant.5.clone.wz_hbm, bf16[4,64,64]{2,1,0:T(8,128)(2,1)} %sk_hbm.1, s32[8]{0:T(128)} %pair_ref.1), custom_call_target="tpu_custom_call" | custom-call | tf_op jit(solution)/shard_map/merge/pallas_call | solution.py:440
  46.1 0.6 %copy.8 = bf16[4,16,64]{2,1,0:T(8,128)(2,1)} copy(bf16[4,16,64]{2,1,0:T(8,128)(2,1)S(1)} %merge.1) | data formatting | bytes 16384

commit v5 on v4

--- a/solution.py
+++ b/solution.py
@@ -278,11 +278,12 @@
                 part_of[2 * me + g, :, LANES:] = y[:, :LANES].astype(BF16)
                 hsend[g, 0] = y[:, LANES:].astype(BF16)
 
-    def make_leaf(q):
+    def leaf_of(q):
         below = jnp.where(sp > 0, hrecv[q, 0].astype(F32), 0.0)
         above = jnp.where(sp < count - 1, hrecv[q, 1].astype(F32), 0.0)
-        leaf[q, :, :LANES] = (part_of[q, :, :LANES].astype(F32) + below).astype(BF16)
-        leaf[q, :, LANES:] = (part_of[q, :, LANES:].astype(F32) + above).astype(BF16)
+        lead = (part_of[q, :, :LANES].astype(F32) + below).astype(BF16)
+        tail = (part_of[q, :, LANES:].astype(F32) + above).astype(BF16)
+        return jnp.concatenate([lead, tail], axis=1)
 
     restrict_group(0)
     small[2].wait()
@@ -300,11 +301,9 @@
     skt[...] = jnp.concatenate([sk_ref[x] for x in range(sk_ref.shape[0])], axis=1)
     for c in early + late:
         c.wait()
-    for q in range(2 * shots):
-        make_leaf(q)
-
-    p0 = leaf[pair_ref[base + 2 * odd]]
-    p1 = leaf[pair_ref[base + 2 * odd + 1]]
+
+    p0 = leaf_of(pair_ref[base + 2 * odd])
+    p1 = leaf_of(pair_ref[base + 2 * odd + 1])
     sk = skt[...]
 
     def scatter(part):
@@ -364,9 +363,11 @@
     m_ref[0, 0:64, :] = nt(p0, jnp.concatenate([p0, sk], axis=0))
     m_ref[0, 64:128, :] = nt(p1, jnp.concatenate([p1, sk], axis=0))
     first = scatter(0)
-    xx = leaf[pair_ref[base + 2 + odd]]
-    q0 = leaf[pair_ref[base]]
-    q1 = leaf[pair_ref[base + 1]]
+    for p in range(2 * shots):
+        leaf[p] = leaf_of(pair_ref[p])
+    xx = leaf[base + 2 + odd]
+    q0 = leaf[base]
+    q1 = leaf[base + 1]
     m_ref[1, 0:64, :] = nt(xx, jnp.concatenate([q0, q1], axis=0))
     m_ref[1, 64:128, :] = jnp.concatenate([nt(p0, p1), nt(p1, p0)], axis=1)
     other = scatter(1)
@@ -413,12 +414,12 @@
     u = u_ref[pl.ds(pl.multiple_of(me * width, width), width), :].astype(BF16)
     total = None
     for p in range(4):
-        term = nn(u[:, RANK * p : RANK * p + RANK], leaf[pair_ref[base + p]])
+        term = nn(u[:, RANK * p : RANK * p + RANK], leaf[base + p])
         total = term if total is None else total + term
     trade.wait()
     v = ur[...]
     for p in range(4):
-        total = total + nn(v[:, RANK * p : RANK * p + RANK], leaf[pair_ref[4 - base + p]])
+        total = total + nn(v[:, RANK * p : RANK * p + RANK], leaf[4 - base + p])
     for i in range(out_ref.shape[0]):
         out_ref[i] = total[:, RANK * i : RANK * i + RANK].astype(BF16)
 

time: 46.8 us -> 46.7 us (level)
  no operation moved by 1% of the time
where the time goes in v5:
time: 46.7 us; the launch traced here: 46.6 us
  Pallas kernels  46 us (99%)
  local copies, waits for them, and re-layouts  0.61 us (1%)
    pallas_call x1, Pallas kernels, body(): pl.pallas_call(functools.partial(kernel, scaling, shots, depth, owners),...  46 us

profile of v5, /device:TPU:1, one launch (start us, length us, event | category | flops | bytes accessed | tf_op | source)
XLA Modules:
  0.0 46.6 jit_solution(16949059770392343436)
XLA Ops:
  0.0 46.0 %merge.1 = bf16[4,16,64]{2,1,0:T(8,128)(2,1)S(1)} custom-call(bf16[2,64,2,128,128]{4,3,2,1,0:T(8,128)(2,1)} %bitcast.2, bf16[2,2,128,128]{3,2,1,0:T(8,128)(2,1)} %bitcast.3, bf16[32,256]{1,0:T(8,128)(2,1)} %constant.4.clone.wxy_hbm, bf16[1024,256]{1,0:T(8,128)(2,1)} %constant.5.clone.wz_hbm, bf16[4,64,64]{2,1,0:T(8,128)(2,1)} %sk_hbm.1, s32[8]{0:T(128)} %pair_ref.1), custom_call_target="tpu_custom_call" | custom-call | tf_op jit(solution)/shard_map/merge/pallas_call | solution.py:441
  46.0 0.6 %copy.8 = bf16[4,16,64]{2,1,0:T(8,128)(2,1)} copy(bf16[4,16,64]{2,1,0:T(8,128)(2,1)S(1)} %merge.1) | data formatting | bytes 16384
